TPU v7x, 32 devices: a whole 2x2x4 slice. The times are simulated.
32 devices in a mesh: wide: 8 (over y, x, core), narrow: 4 (over z).
Axes of the slice: x: 2, y: 2, z: 4, core: 2. Of those that a mesh axis runs over, the one named last changes fastest.
Arguments:
- hidden: bfloat16 [1024, 4096], P('wide', 'narrow'), may hold values from -6 to 6
- head_weight: bfloat16 [32768, 4096], P('wide', 'narrow'), may hold values from -0.25 to 0.25
- lse: float32 [1024], replicated, may hold values from 12 to 14
- targets: int32 [1024], replicated, may hold values from 0 to 32767
- loss_weight: float32 [1024], replicated, may hold values from 16 to 48
- block_tiles: int32 [8, 8, 4], P(None, 'wide'), may hold values from 0 to 31, as said below
- block_counts: int32 [8, 8], P(None, 'wide'), may hold values from 0 to 4, as said below
- gate_pre: bfloat16 [1024, 7168], P('wide', 'narrow'), may hold values from -6 to 6
- up_pre: bfloat16 [1024, 7168], P('wide', 'narrow'), may hold values from -6 to 6
- down_weight: bfloat16 [7168, 4096], P('narrow'), may hold values from -0.0625 to 0.0625
Outputs:
- head_grad: bfloat16 [1024, 4096], P('wide', 'narrow')
- gate_grad: bfloat16 [1024, 7168], P('wide', 'narrow')
- up_grad: bfloat16 [1024, 7168], P('wide', 'narrow')
Inputs may be any that keep to these rules, and one draw needn't show every extreme that they name: The first block_counts[b, s] entries of block_tiles[b, s] are distinct; the other entries are ignored. `block_counts`: some row block has 4 active tiles in some shard; one shard has exactly 16 active tiles over all row blocks, and no shard has more.
All inputs are finite; a program needn't handle non-finite values.
Results may differ from a plain program's by a relative error of at most 0.0035.
The roundings to bfloat16 on the way count: a program that leaves them out, or rounds other values in their place, can miss the bound.
Values may be sent and summed in bfloat16 or wider, within the bound.
No kernel may reach another device: no remote copies, remote signals or barrier semaphores. Data moves between devices by JAX's collectives and lax.ppermute only.
A program may use at most 128 MiB of HBM per device.

v0:
```python
import jax
import jax.numpy as jnp
from jax import lax
from jax.sharding import PartitionSpec as P

TILE = 128


def slot_table(tiles_here, counts_here, slot_count):
    block_total, per_block = tiles_here.shape
    slot_live = (jnp.arange(per_block, dtype=jnp.int32)[None, :] < counts_here[:, None]).reshape(-1)
    position = jnp.cumsum(slot_live.astype(jnp.int32)) - 1
    select = (position[None, :] == jnp.arange(slot_count, dtype=jnp.int32)[:, None]) & slot_live[
        None, :
    ]
    chosen = select.astype(jnp.int32)
    block_ids = jnp.repeat(jnp.arange(block_total, dtype=jnp.int32), per_block)
    slot_blocks = jnp.sum(chosen * block_ids[None, :], axis=1)
    slot_tiles = jnp.sum(chosen * tiles_here.reshape(-1)[None, :], axis=1)
    return (slot_blocks, slot_tiles, jnp.sum(chosen, axis=1) > 0)


def cell_weights(logits, lse_rows, scale_rows, slot_live):
    scaled = jnp.exp(logits - lse_rows[:, :, None]) * scale_rows[:, :, None]
    return jnp.where(slot_live[:, None, None], scaled, 0.0).astype(jnp.bfloat16)


def on_device(
    hidden,
    head_weight,
    lse,
    targets,
    loss_weight,
    block_tiles,
    block_counts,
    gate_pre,
    up_pre,
    down_weight,
):
    features = hidden.shape[1]
    row_count = hidden.shape[0]
    vocab_here = head_weight.shape[0]
    offset = lax.axis_index("wide") * vocab_here
    gathered = lax.all_gather(hidden, "wide", axis=0, tiled=True)
    blocks = gathered.shape[0] // TILE
    weight_tiles = head_weight.reshape(vocab_here // TILE, TILE, features)
    tiles_here = block_tiles[:, 0, :]
    counts_here = block_counts[:, 0]
    per_block = tiles_here.shape[1]
    lse_blocks = lse.reshape(blocks, TILE)
    scale_blocks = loss_weight.reshape(blocks, TILE)
    slot_count = blocks // 2 * per_block
    slot_blocks, slot_tiles, slot_live = slot_table(tiles_here, counts_here, slot_count)
    picked = jnp.take(weight_tiles, slot_tiles, axis=0)
    row_blocks = jnp.take(gathered.reshape(blocks, TILE, features), slot_blocks, axis=0)
    partial_value = jnp.einsum(
        "srd,scd->src", row_blocks, picked, preferred_element_type=jnp.float32
    )
    slot_lse = jnp.take(lse_blocks, slot_blocks, axis=0)
    slot_scale = jnp.take(scale_blocks, slot_blocks, axis=0)
    logits = lax.psum(partial_value, "narrow")
    cell_probs = cell_weights(logits, slot_lse, slot_scale, slot_live)
    contrib = jnp.einsum("src,scd->srd", cell_probs, picked, preferred_element_type=jnp.float32)
    contrib = contrib.reshape(slot_count, TILE * features)
    block_span = row_count * lax.axis_size("wide") // TILE
    wanted = jnp.arange(block_span, dtype=jnp.int32)
    member = ((slot_blocks[None, :] == wanted[:, None]) & slot_live[None, :]).astype(jnp.float32)
    softmax_part = jnp.dot(
        member, contrib, precision=lax.Precision.HIGHEST, preferred_element_type=jnp.float32
    ).reshape(row_count * lax.axis_size("wide"), features)
    local_ids = targets - offset
    inside = (local_ids >= 0) & (local_ids < vocab_here)
    target_rows = jnp.take(head_weight, jnp.clip(local_ids, 0, vocab_here - 1), axis=0).astype(
        jnp.float32
    )
    factor = jnp.where(inside, loss_weight, 0.0)
    head_grad = lax.psum_scatter(
        softmax_part - factor[:, None] * target_rows, "wide", scatter_dimension=0, tiled=True
    ).astype(jnp.bfloat16)
    unit_grad = lax.dot_general(
        lax.all_gather(head_grad, "narrow", axis=1, tiled=True),
        down_weight,
        (((1,), (1,)), ((), ())),
        preferred_element_type=jnp.float32,
    )
    gate_value = gate_pre.astype(jnp.float32)
    up_value = up_pre.astype(jnp.float32)
    gate_sig = jax.nn.sigmoid(gate_value)
    up_grad = (unit_grad * gate_value * gate_sig).astype(jnp.bfloat16)
    gate_grad = (unit_grad * up_value * gate_sig * (1.0 + gate_value * (1.0 - gate_sig))).astype(
        jnp.bfloat16
    )
    return (head_grad, gate_grad, up_grad)


def solution(mesh):
    in_specs = (
        P("wide", "narrow"),
        P("wide", "narrow"),
        P(),
        P(),
        P(),
        P(None, "wide", None),
        P(None, "wide"),
        P("wide", "narrow"),
        P("wide", "narrow"),
        P("narrow", None),
    )
    out_specs = (P("wide", "narrow"), P("wide", "narrow"), P("wide", "narrow"))
    return jax.shard_map(
        on_device, mesh=mesh, in_specs=in_specs, out_specs=out_specs, check_vma=False
    )
```

profile of v0, /device:TPU:0, one launch (start us, length us, event | category | flops | bytes accessed | tf_op | source)
XLA Modules:
  0.0 223.7 jit_solution(11905009591479860913)
XLA Ops:
  7.2 0.0 all-gather.3.cloned.1.call-start
  7.2 0.7 all-gather.3.cloned.1.call-update
  7.9 0.0 all-reduce.2.cloned.1.call-start
  8.0 0.7 iota_compare_fusion.2
  8.7 0.1 reshape.201
  8.8 0.1 lt.82
  8.9 0.1 mul.57
  8.9 0.8 copy.18
  9.7 0.1 mul.60
  9.8 0.1 reduce-window.8
  9.8 0.1 add_reduce_fusion
  10.0 0.2 convert_reduce_fusion
  10.1 0.6 gather_fusion.3
  10.7 1.2 gather_fusion.4
  12.0 6.1 %gather_fusion.1 = bf16[16,128,1024]{2,1,0:T(8,128)(2,1)} fusion(bf16[32,128,1024]{2,1,0:T(8,128)(2,1)} %bitcast.21, s32[1024]{0:T(1024)S(1)} %pad_clamp_fusion.1), kind=kCustom, calls=%fused_computation.3 | custom fusion | bytes 8388672 | tf_op jit(solution)/shard_map/jit(_take)/gather | solution.py:54
  18.1 22.3 %all-gather.3.cloned.1.call-done = bf16[1024,1024]{1,0:T(8,128)(2,1)} async-done(((bf16[128,1024]{1,0:T(8,128)(2,1)}), bf16[1024,1024]{1,0:T(8,128)(2,1)}) %all-gather.3.cloned.1.call-update) | async-done | bytes 2097168 | tf_op jit(solution)/shard_map/all_gather | solution.py:44
  40.4 4.4 %gather_fusion = bf16[16,128,1024]{2,1,0:T(8,128)(2,1)} fusion(bf16[8,128,1024]{2,1,0:T(8,128)(2,1)} %bitcast.24, s32[1024]{0:T(1024)S(1)} %pad_clamp_fusion.2), kind=kCustom, calls=%fused_computation.2 | custom fusion | bytes 8388672 | tf_op jit(solution)/shard_map/jit(_take)/gather | solution.py:55
  44.8 6.0 %fusion = f32[16,128,128]{2,1,0:T(8,128)} fusion(bf16[16,128,1024]{2,1,0:T(8,128)(2,1)} %gather_fusion, pred[16]{0:T(512)(128)(4,1)S(1)} %get-tuple-element.14, bf16[16,128,1024]{2,1,0:T(8,128)(2,1)} %gather_fusion.1, pred[16]{0:T(512)(128)(4,1)S(1)} %get-tuple-element.13), kind=kOutput, calls=%fused_computation.6 | convolution fusion | flops 541065216 | bytes 9437216 | tf_op jit(solution)/shard_map/srd,scd->src/dot_general | solution.py:56
  50.8 0.2 reduce-scatter.2.cloned.1.call-start
  51.1 9.4 %gather_fusion.2 = bf16[1024,1024]{1,0:T(8,128)(2,1)S(1)} fusion(bf16[4096,1024]{1,0:T(8,128)(2,1)} %param.13, s32[1024]{0:T(1024)S(1)} %fusion.21), kind=kCustom, calls=%fused_computation.4 | custom fusion | bytes 4198400 | tf_op jit(solution)/shard_map/jit(_take)/gather | solution.py:73
  60.6 0.1 broadcast_select_fusion.4
  60.7 42.2 %all-reduce.2.cloned.1.call-done = f32[16,128,128]{2,1,0:T(8,128)} async-done(((f32[16,128,128]{2,1,0:T(8,128)}), f32[16,128,128]{2,1,0:T(8,128)}) %all-reduce.2.cloned.1.call-update) | async-done | bytes 1048592 | tf_op jit(solution)/shard_map/psum | solution.py:61
  102.9 3.8 %fusion.4 = f32[16,128,1024]{2,1,0:T(8,128)S(1)} fusion(bf16[16,128,1024]{2,1,0:T(8,128)(2,1)} %gather_fusion.1, pred[16]{0:T(512)(128)(4,1)S(1)} %get-tuple-element.13, f32[16,128,128]{2,1,0:T(8,128)} %all-reduce.2.cloned.1.call-done, f32[16,128]{1,0:T(8,128)S(1)} %get-tuple-element.10, f32[16,128]{1,0:T(8,128)S(1)} %get-tuple-element.9, ...), kind=kOutput, calls=%fused_computation.11 | convolution fusion | flops 540016640 | bytes 13647904 | tf_op jit(solution)/shard_map/src,scd->srd/dot_general | solution.py:63
  106.7 4.9 %copy.19 = f32[2,8,128,1024]{3,1,2,0:T(8,128)S(1)} copy(f32[2,8,128,1024]{3,2,1,0:T(8,128)S(1)} %bitcast.22) | data formatting | bytes 16777216
  111.6 4.4 %fusion.19 = f32[8,131072]{1,0:T(8,128)} fusion(f32[16,131072]{1,0:T(8,128)S(1)} %bitcast.23, s32[16]{0:T(128)S(1)} %get-tuple-element.6, pred[16]{0:T(512)(128)(4,1)S(1)} %broadcast_compare_fusion), kind=kOutput, calls=%fused_computation.43 | convolution fusion | flops 201326848 | bytes 12582992 | tf_op jit(solution)/shard_map/dot_general | solution.py:68
  116.0 4.9 %reshape.152 = f32[1024,1024]{1,0:T(8,128)} reshape(f32[8,131072]{1,0:T(8,128)} %fusion.19) | data formatting | bytes 8388608 | tf_op jit(solution)/shard_map/reshape | solution.py:70
  120.9 4.1 %multiply_subtract_fusion = f32[1024,1024]{1,0:T(8,128)} fusion(f32[1024,1024]{1,0:T(8,128)} %reshape.152, bf16[1024,1024]{1,0:T(8,128)(2,1)S(1)} %gather_fusion.2, f32[1024]{0:T(1024)S(1)} %and_select_fusion, pred[1024]{0:T(1024)(128)(4,1)S(1)} %compare_and_fusion), kind=kLoop, calls=%fused_computation.5 | loop fusion | flops 4194304 | bytes 10490880 | tf_op jit(solution)/shard_map/sub | solution.py:78
  125.0 0.3 all-gather.5.cloned.1.call-start
  125.3 50.3 %reduce-scatter.2.cloned.1.call-done = f32[128,1024]{1,0:T(8,128)} async-done(((f32[1024,1024]{1,0:T(8,128)}), f32[128,1024]{1,0:T(8,128)}) %reduce-scatter.2.cloned.1.call-update) | async-done | bytes 524304 | tf_op jit(solution)/shard_map/reduce_scatter | solution.py:77
  175.6 1.8 convert_element_type.45
  177.4 28.2 %all-gather.5.cloned.1.call-done = bf16[128,4096]{1,0:T(8,128)(2,1)} async-done(((bf16[128,1024]{1,0:T(8,128)(2,1)}), bf16[128,4096]{1,0:T(8,128)(2,1)}) %all-gather.5.cloned.1.call-update) | async-done | bytes 1048592 | tf_op jit(solution)/shard_map/all_gather | solution.py:81
  205.6 11.5 %fusion.12 = (bf16[128,1792]{1,0:T(8,128)(2,1)}, bf16[128,1792]{1,0:T(8,128)(2,1)}) fusion(bf16[128,1792]{1,0:T(8,128)(2,1)S(1)} %copy-done.4, bf16[128,1792]{1,0:T(8,128)(2,1)S(1)} %copy-done.5, bf16[128,4096]{1,0:T(8,128)(2,1)} %all-gather.5.cloned.1.call-done, bf16[1792,4096]{1,0:T(8,128)(2,1)} %param.21), kind=kOutput, calls=%fused_computation.23 | convolution fusion | flops 1882488832 | bytes 17563648 | tf_op jit(solution)/shard_map/dot_general | solution.py:80
  (27 shorter events, 0.2 us)
Async XLA Ops:
  7.2 3.0 %copy-start = (f32[1024]{0:T(1024)S(1)}, f32[1024]{0:T(1024)}, u32[]{:S(2)}) copy-start(f32[1024]{0:T(1024)} %param.14) | copy-start | bytes 12292
  7.2 33.2 %all-gather.3.cloned.1.call-start = ((), (), s32[]{:S(2)}) async-start(), calls=%async_computation.1 | async-start | bytes 2359296 | tf_op jit(solution)/shard_map/all_gather | solution.py:44
  7.9 95.0 %all-reduce.2.cloned.1.call-start = ((), (), s32[]{:S(2)}) async-start(), calls=%async_computation.2 | async-start | bytes 2097152 | tf_op jit(solution)/shard_map/psum | solution.py:61
  44.8 6.3 %copy-start.3 = (s32[1024]{0:T(1024)S(1)}, s32[1024]{0:T(1024)}, u32[]{:S(2)}) copy-start(s32[1024]{0:T(1024)} %param.15) | copy-start | bytes 12292
  50.8 124.7 %reduce-scatter.2.cloned.1.call-start = ((), (), s32[]{:S(2)}) async-start(), calls=%async_computation.3 | async-start | bytes 4718592 | tf_op jit(solution)/shard_map/reduce_scatter | solution.py:77
  51.1 9.5 %copy-start.2 = (f32[1024]{0:T(1024)S(1)}, f32[1024]{0:T(1024)}, u32[]{:S(2)}) copy-start(f32[1024]{0:T(1024)} %param.16) | copy-start | bytes 12292
  125.0 80.6 %copy-start.4 = (bf16[128,1792]{1,0:T(8,128)(2,1)S(1)}, bf16[128,1792]{1,0:T(8,128)(2,1)}, u32[]{:S(2)}) copy-start(bf16[128,1792]{1,0:T(8,128)(2,1)} %param.19) | copy-start | bytes 1376260
  125.0 80.6 %copy-start.5 = (bf16[128,1792]{1,0:T(8,128)(2,1)S(1)}, bf16[128,1792]{1,0:T(8,128)(2,1)}, u32[]{:S(2)}) copy-start(bf16[128,1792]{1,0:T(8,128)(2,1)} %param.20) | copy-start | bytes 1376260
  125.0 80.6 %all-gather.5.cloned.1.call-start = ((), (), s32[]{:S(2)}) async-start(), calls=%async_computation.4 | async-start | bytes 1310720 | tf_op jit(solution)/shard_map/all_gather | solution.py:81
  205.6 11.5 %copy-start.1 = (f32[1024]{0:T(1024)S(1)}, f32[1024]{0:T(1024)}, u32[]{:S(2)}) copy-start(f32[1024]{0:T(1024)} %param.14) | copy-start | bytes 12292
Sparse Core Ops, SparseCore 0:
  9.9 30.4 all-gather.2
  50.9 51.8 all-reduce.1
  125.1 50.4 reduce-scatter.1
  177.6 27.9 all-gather.4
where the time goes:
time: 224 us
  waiting for transfers between devices  144 us (64%)
  local copies, waits for them, and re-layouts  32.6 us (15%)
  matrix products  25.8 us (12%)
  between operations  13.9 us (6%)
  other arithmetic  7.04 us (3%)
    reduce_scatter x1, waiting for transfers between devices, on_device(): lax.psum_scatter(softmax_part - factor[:, None] * target_rows, 'wide', sc...  50.3 us
    psum x1, waiting for transfers between devices, on_device(): logits = lax.psum(partial_value, 'narrow')  42.2 us
    all_gather x1, waiting for transfers between devices, on_device(): lax.all_gather(head_grad, 'narrow', axis=1, tiled=True)  28.2 us
    all_gather x1, waiting for transfers between devices, on_device(): gathered = lax.all_gather(hidden, 'wide', axis=0, tiled=True)  22.3 us
    dot_general x1, matrix products, on_device(): lax.dot_general(lax.all_gather(head_grad, 'narrow', axis=1, tiled=True),...  11.5 us
    gather x1, local copies, waits for them, and re-layouts, on_device(): jnp.take(head_weight, jnp.clip(local_ids, 0, vocab_here - 1), axis=0)  9.44 us
    gather x1, local copies, waits for them, and re-layouts, on_device(): picked = jnp.take(weight_tiles, slot_tiles, axis=0)  6.13 us
    dot_general x1, matrix products, on_device(): jnp.einsum('srd,scd->src', row_blocks, picked, preferred_element_type=jnp...  6 us
  transfers between devices with their start and end apart: 4, of which 4 were waited for; matrix products, arithmetic and copies ran while one was open for 9% of the time, Pallas kernels for 0%

commit v1 on v0

--- a/solution.py
+++ b/solution.py
@@ -58,7 +58,9 @@
     )
     slot_lse = jnp.take(lse_blocks, slot_blocks, axis=0)
     slot_scale = jnp.take(scale_blocks, slot_blocks, axis=0)
-    logits = lax.psum(partial_value, "narrow")
+    logits = partial_value
+    for hop in (1, 2):
+        logits = logits + lax.ppermute(logits, "narrow", [(dev, dev ^ hop) for dev in range(4)])
     cell_probs = cell_weights(logits, slot_lse, slot_scale, slot_live)
     contrib = jnp.einsum("src,scd->srd", cell_probs, picked, preferred_element_type=jnp.float32)
     contrib = contrib.reshape(slot_count, TILE * features)

time: 224 us -> 245 us (1.094)
  waiting for transfers between devices: 144 us -> 163 us
  starting transfers between devices: 0.56 us -> 4.36 us
    ppermute x0 -> x2, waiting for transfers between devices: none -> 58.4 us  [on_device(): lax.ppermute(logits, 'narrow', [(dev, dev ^ hop) for dev in range(4)])]
    psum x1 -> x0, waiting for transfers between devices: 42.2 us -> none  [on_device(): logits = lax.psum(partial_value, 'narrow')]
    ppermute x0 -> x2, starting transfers between devices: none -> 4.02 us  [on_device(): lax.ppermute(logits, 'narrow', [(dev, dev ^ hop) for dev in range(4)])]
  transfers between devices with their start and end apart: 4 -> 5, of which waited for: 4 -> 5; matrix products, arithmetic and copies ran while one was open for 9% -> 8% of each run, Pallas kernels for 0% -> 0%
where the time goes in v1:
time: 245 us
  waiting for transfers between devices  163 us (67%)
  local copies, waits for them, and re-layouts  32.1 us (13%)
  matrix products  24.8 us (10%)
  between operations  13.9 us (6%)
  other arithmetic  7.15 us (3%)
  starting transfers between devices  4.36 us (2%)
    ppermute x2, waiting for transfers between devices, on_device(): lax.ppermute(logits, 'narrow', [(dev, dev ^ hop) for dev in range(4)])  58.4 us
    reduce_scatter x1, waiting for transfers between devices, on_device(): lax.psum_scatter(softmax_part - factor[:, None] * target_rows, 'wide', sc...  51 us
    all_gather x1, waiting for transfers between devices, on_device(): lax.all_gather(head_grad, 'narrow', axis=1, tiled=True)  28.3 us
    all_gather x1, waiting for transfers between devices, on_device(): gathered = lax.all_gather(hidden, 'wide', axis=0, tiled=True)  24.1 us
    dot_general x1, matrix products, on_device(): lax.dot_general(lax.all_gather(head_grad, 'narrow', axis=1, tiled=True),...  11.5 us
    gather x1, local copies, waits for them, and re-layouts, on_device(): jnp.take(head_weight, jnp.clip(local_ids, 0, vocab_here - 1), axis=0)  9.62 us
    gather x1, local copies, waits for them, and re-layouts, on_device(): picked = jnp.take(weight_tiles, slot_tiles, axis=0)  6.14 us
    unnamed x14, local copies, waits for them, and re-layouts  5.65 us
  transfers between devices with their start and end apart: 5, of which 5 were waited for; matrix products, arithmetic and copies ran while one was open for 8% of the time, Pallas kernels for 0%

profile of v1, /device:TPU:0, one launch (start us, length us, event | category | flops | bytes accessed | tf_op | source)
XLA Modules:
  0.0 244.9 jit_solution(18208855697398647666)
XLA Ops:
  7.2 0.7 all-gather.3.cloned.1.call-update
  8.0 0.7 iota_compare_fusion.2
  8.7 0.1 reshape.201
  8.8 0.1 lt.82
  8.9 0.1 mul.57
  8.9 0.8 copy.18
  9.7 0.1 mul.60
  9.8 0.1 add_reduce_fusion
  9.9 0.2 convert_reduce_fusion
  10.1 6.1 %gather_fusion.1 = bf16[16,128,1024]{2,1,0:T(8,128)(2,1)} fusion(bf16[32,128,1024]{2,1,0:T(8,128)(2,1)} %bitcast.21, s32[1024]{0:T(1024)S(1)} %pad_clamp_fusion.1), kind=kCustom, calls=%fused_computation.3 | custom fusion | bytes 8388672 | tf_op jit(solution)/shard_map/jit(_take)/gather | solution.py:54
  16.3 24.1 %all-gather.3.cloned.1.call-done = bf16[1024,1024]{1,0:T(8,128)(2,1)} async-done(((bf16[128,1024]{1,0:T(8,128)(2,1)}), bf16[1024,1024]{1,0:T(8,128)(2,1)}) %all-gather.3.cloned.1.call-update) | async-done | bytes 2097168 | tf_op jit(solution)/shard_map/all_gather | solution.py:44
  40.4 4.4 %gather_fusion = bf16[16,128,1024]{2,1,0:T(8,128)(2,1)} fusion(bf16[8,128,1024]{2,1,0:T(8,128)(2,1)} %bitcast.24, s32[1024]{0:T(1024)S(1)} %pad_clamp_fusion.2), kind=kCustom, calls=%fused_computation.2 | custom fusion | bytes 8388672 | tf_op jit(solution)/shard_map/jit(_take)/gather | solution.py:55
  44.8 5.0 %fusion = f32[16,128,128]{2,1,0:T(8,128)S(1)} fusion(bf16[16,128,1024]{2,1,0:T(8,128)(2,1)} %gather_fusion, pred[16]{0:T(512)(128)(4,1)S(1)} %get-tuple-element.14, bf16[16,128,1024]{2,1,0:T(8,128)(2,1)} %gather_fusion.1, pred[16]{0:T(512)(128)(4,1)S(1)} %get-tuple-element.13), kind=kOutput, calls=%fused_computation.6 | convolution fusion | flops 541065216 | bytes 9437216 | tf_op jit(solution)/shard_map/srd,scd->src/dot_general | solution.py:56
  49.7 1.6 collective-permute-start
  51.3 0.6 gather_fusion.3
  51.9 0.6 gather_fusion.4
  52.5 22.6 %collective-permute-done = f32[16,128,128]{2,1,0:T(8,128)S(1)} collective-permute-done((f32[16,128,128]{2,1,0:T(8,128)S(1)}, f32[16,128,128]{2,1,0:T(8,128)S(1)}, u32[]{:S(2)}, u32[]{:S(2)}) %collective-permute-start) | collective-permute-done | bytes 1048608 | tf_op jit(solution)/shard_map/ppermute | solution.py:63
  75.1 0.1 add.63
  75.2 2.5 %collective-permute-start.1 = (f32[16,128,128]{2,1,0:T(8,128)S(1)}, f32[16,128,128]{2,1,0:T(8,128)}, u32[]{:S(2)}, u32[]{:S(2)}) collective-permute-start(f32[16,128,128]{2,1,0:T(8,128)S(1)} %add.63), channel_id=1, source_target_pairs={{0,2},{1,3},{2,0},{3,1},{4,6},{5,7},{6,4},{7,5},{8,10},{9,11},{10,... | collective-permute-start | bytes 3145736 | tf_op jit(solution)/shard_map/ppermute | solution.py:63
  77.7 9.6 %gather_fusion.2 = bf16[1024,1024]{1,0:T(8,128)(2,1)S(1)} fusion(bf16[4096,1024]{1,0:T(8,128)(2,1)} %param.13, s32[1024]{0:T(1024)S(1)} %fusion.21), kind=kCustom, calls=%fused_computation.4 | custom fusion | bytes 4198400 | tf_op jit(solution)/shard_map/jit(_take)/gather | solution.py:75
  87.4 0.1 broadcast_select_fusion.4
  87.5 35.8 %collective-permute-done.1 = f32[16,128,128]{2,1,0:T(8,128)} collective-permute-done((f32[16,128,128]{2,1,0:T(8,128)S(1)}, f32[16,128,128]{2,1,0:T(8,128)}, u32[]{:S(2)}, u32[]{:S(2)}) %collective-permute-start.1) | collective-permute-done | bytes 1048608 | tf_op jit(solution)/shard_map/ppermute | solution.py:63
  123.2 3.9 %fusion.4 = f32[16,128,1024]{2,1,0:T(8,128)S(1)} fusion(bf16[16,128,1024]{2,1,0:T(8,128)(2,1)} %gather_fusion.1, pred[16]{0:T(512)(128)(4,1)S(1)} %get-tuple-element.13, f32[16,128,128]{2,1,0:T(8,128)S(1)} %add.63, f32[16,128,128]{2,1,0:T(8,128)} %collective-permute-done.1, f32[16,128]{1,0:T(8,128)S(1)} %get-tuple-element.10, ...), kind=kOutput, calls=%fused_computation.11 | convolution fusion | flops 540278784 | bytes 14696480 | tf_op jit(solution)/shard_map/src,scd->srd/dot_general | solution.py:65
  127.1 4.9 %copy.19 = f32[2,8,128,1024]{3,1,2,0:T(8,128)S(1)} copy(f32[2,8,128,1024]{3,2,1,0:T(8,128)S(1)} %bitcast.22) | data formatting | bytes 16777216
  132.0 4.4 %fusion.19 = f32[8,131072]{1,0:T(8,128)} fusion(f32[16,131072]{1,0:T(8,128)S(1)} %bitcast.23, s32[16]{0:T(128)S(1)} %get-tuple-element.6, pred[16]{0:T(512)(128)(4,1)S(1)} %broadcast_compare_fusion), kind=kOutput, calls=%fused_computation.43 | convolution fusion | flops 201326848 | bytes 12582992 | tf_op jit(solution)/shard_map/dot_general | solution.py:70
  136.4 4.9 %reshape.152 = f32[1024,1024]{1,0:T(8,128)} reshape(f32[8,131072]{1,0:T(8,128)} %fusion.19) | data formatting | bytes 8388608 | tf_op jit(solution)/shard_map/reshape | solution.py:72
  141.3 4.0 %multiply_subtract_fusion = f32[1024,1024]{1,0:T(8,128)} fusion(f32[1024,1024]{1,0:T(8,128)} %reshape.152, bf16[1024,1024]{1,0:T(8,128)(2,1)S(1)} %gather_fusion.2, f32[1024]{0:T(1024)S(1)} %and_select_fusion, pred[1024]{0:T(1024)(128)(4,1)S(1)} %compare_and_fusion), kind=kLoop, calls=%fused_computation.5 | loop fusion | flops 4194304 | bytes 10490880 | tf_op jit(solution)/shard_map/sub | solution.py:80
  145.4 0.3 all-gather.5.cloned.1.call-start
  145.6 51.0 %reduce-scatter.2.cloned.1.call-done = f32[128,1024]{1,0:T(8,128)} async-done(((f32[1024,1024]{1,0:T(8,128)}), f32[128,1024]{1,0:T(8,128)}) %reduce-scatter.2.cloned.1.call-update) | async-done | bytes 524304 | tf_op jit(solution)/shard_map/reduce_scatter | solution.py:79
  196.7 1.8 convert_element_type.45
  198.5 28.3 %all-gather.5.cloned.1.call-done = bf16[128,4096]{1,0:T(8,128)(2,1)} async-done(((bf16[128,1024]{1,0:T(8,128)(2,1)}), bf16[128,4096]{1,0:T(8,128)(2,1)}) %all-gather.5.cloned.1.call-update) | async-done | bytes 1048592 | tf_op jit(solution)/shard_map/all_gather | solution.py:83
  226.8 11.5 %fusion.12 = (bf16[128,1792]{1,0:T(8,128)(2,1)}, bf16[128,1792]{1,0:T(8,128)(2,1)}) fusion(bf16[128,1792]{1,0:T(8,128)(2,1)S(1)} %copy-done.4, bf16[128,1792]{1,0:T(8,128)(2,1)S(1)} %copy-done.5, bf16[128,4096]{1,0:T(8,128)(2,1)} %all-gather.5.cloned.1.call-done, bf16[1792,4096]{1,0:T(8,128)(2,1)} %param.21), kind=kOutput, calls=%fused_computation.23 | convolution fusion | flops 1882488832 | bytes 17563648 | tf_op jit(solution)/shard_map/dot_general | solution.py:82
  (29 shorter events, 0.3 us)
Async XLA Ops:
  7.2 44.2 %copy-start = (f32[1024]{0:T(1024)S(1)}, f32[1024]{0:T(1024)}, u32[]{:S(2)}) copy-start(f32[1024]{0:T(1024)} %param.14) | copy-start | bytes 12292
  7.2 33.2 %all-gather.3.cloned.1.call-start = ((), (), s32[]{:S(2)}) async-start(), calls=%async_computation.1 | async-start | bytes 2359296 | tf_op jit(solution)/shard_map/all_gather | solution.py:44
  7.9 188.7 %reduce-scatter.2.cloned.1.call-start = ((), (), s32[]{:S(2)}) async-start(), calls=%async_computation.2 | async-start | bytes 4718592 | tf_op jit(solution)/shard_map/reduce_scatter | solution.py:79
  44.8 7.1 %copy-start.2 = (f32[1024]{0:T(1024)S(1)}, f32[1024]{0:T(1024)}, u32[]{:S(2)}) copy-start(f32[1024]{0:T(1024)} %param.16) | copy-start | bytes 12292
  44.8 32.9 %copy-start.3 = (s32[1024]{0:T(1024)S(1)}, s32[1024]{0:T(1024)}, u32[]{:S(2)}) copy-start(s32[1024]{0:T(1024)} %param.15) | copy-start | bytes 12292
  49.7 25.4 %collective-permute-start = (f32[16,128,128]{2,1,0:T(8,128)S(1)}, f32[16,128,128]{2,1,0:T(8,128)S(1)}, u32[]{:S(2)}, u32[]{:S(2)}) collective-permute-start(f32[16,128,128]{2,1,0:T(8,128)S(1)} %fusion), channel_id=1, source_target_pairs={{0,1},{1,0},{2,3},{3,2},{4,5},{5,4},{6,7},{7,6},{8,9},{9,8},{10,11... | collective-permute-start | bytes 3145736 | tf_op jit(solution)/shard_map/ppermute | solution.py:63
  75.2 48.0 %collective-permute-start.1 = (f32[16,128,128]{2,1,0:T(8,128)S(1)}, f32[16,128,128]{2,1,0:T(8,128)}, u32[]{:S(2)}, u32[]{:S(2)}) collective-permute-start(f32[16,128,128]{2,1,0:T(8,128)S(1)} %add.63), channel_id=1, source_target_pairs={{0,2},{1,3},{2,0},{3,1},{4,6},{5,7},{6,4},{7,5},{8,10},{9,11},{10,... | collective-permute-start | bytes 3145736 | tf_op jit(solution)/shard_map/ppermute | solution.py:63
  145.3 81.5 %copy-start.4 = (bf16[128,1792]{1,0:T(8,128)(2,1)S(1)}, bf16[128,1792]{1,0:T(8,128)(2,1)}, u32[]{:S(2)}) copy-start(bf16[128,1792]{1,0:T(8,128)(2,1)} %param.19) | copy-start | bytes 1376260
  145.3 81.5 %copy-start.5 = (bf16[128,1792]{1,0:T(8,128)(2,1)S(1)}, bf16[128,1792]{1,0:T(8,128)(2,1)}, u32[]{:S(2)}) copy-start(bf16[128,1792]{1,0:T(8,128)(2,1)} %param.20) | copy-start | bytes 1376260
  145.4 81.4 %all-gather.5.cloned.1.call-start = ((), (), s32[]{:S(2)}) async-start(), calls=%async_computation.3 | async-start | bytes 1310720 | tf_op jit(solution)/shard_map/all_gather | solution.py:83
  226.8 11.5 %copy-start.1 = (f32[1024]{0:T(1024)S(1)}, f32[1024]{0:T(1024)}, u32[]{:S(2)}) copy-start(f32[1024]{0:T(1024)} %param.14) | copy-start | bytes 12292
Sparse Core Ops, SparseCore 0:
  9.9 30.4 all-gather.2
  145.5 51.1 reduce-scatter.1
  198.8 27.9 all-gather.4
